TPU v7x, 32 devices: a whole 2x2x4 slice. The times are simulated.
32 devices in a mesh: row: 16 (over z, y, core), col: 2 (over x).
Axes of the slice: x: 2, y: 2, z: 4, core: 2. Of those that a mesh axis runs over, the one named last changes fastest.
Arguments:
- seq: float32 [768, 1024], P('row', 'col'), may hold values from -6 to 6
- query: float32 [768, 1024], P('row', 'col'), may hold values from -24 to 24, as said below
- key: float32 [768, 1024], P('col', 'row'), may hold values from -24 to 24, as said below
- value: float32 [768, 1024], P('col', 'row'), may hold values from -6 to 6
- pair: float32 [768, 768, 128], P('row', 'col'), may hold values from -6 to 6
- w_bias: float32 [128, 32], replicated, may hold values from -0.5 to 0.5
- w_out: float32 [1024, 1024], P(None, 'col'), may hold values from -0.75 to 0.75
- w_left: float32 [1024, 64], P('col'), may hold values from -0.1875 to 0.1875
- w_right: float32 [1024, 64], P('col'), may hold values from -0.1875 to 0.1875
- w_outer: float32 [128, 128], replicated, may hold values from -0.5 to 0.5
- outer_bias: float32 [128], replicated, may hold values from -3 to 3
- w_up: float32 [128, 512], replicated, may hold values from -0.5 to 0.5
- w_down: float32 [512, 128], replicated, may hold values from -0.25 to 0.25
Outputs:
- seq_new: float32 [768, 1024], P('row', 'col')
- pair_new: float32 [768, 768, 128], P('row', 'col')
Inputs may be any that keep to these rules, and one draw needn't show every extreme that they name: `query`: Head-major queries of order one; some residues may be much larger. `key`: Head-major keys of order one; some residues may be much larger.
All inputs are finite; a program needn't handle non-finite values.
Results may differ from a plain program's by a relative error of at most 0.0003.
Values sent between devices are 32-bit elements; how exact they have to be, the bound alone decides.
A program may use at most 128 MiB of HBM per device.

v0:
```python
import jax
import jax.numpy as jnp
from jax import lax
from jax.sharding import PartitionSpec as P

HIGH = lax.Precision.HIGHEST


def merged(x, axis, combine):
    everything = jax.tree.map(lambda part: lax.all_gather(part, axis), x)
    leading = jax.tree.map(lambda part: part[0], everything)

    def hop(k, so_far):
        return combine(so_far, jax.tree.map(lambda part: part[k], everything))

    return lax.fori_loop(1, lax.axis_size(axis), hop, leading)


def channel_norm(x):
    centre = x - jnp.mean(x, axis=-1, keepdims=True)
    return centre * lax.rsqrt(jnp.mean(centre * centre, axis=-1, keepdims=True) + 1e-05)


def combine(first, second):
    top = jnp.maximum(first[0], second[0])
    scale_one = jnp.exp(first[0] - top)
    scale_two = jnp.exp(second[0] - top)
    totals = first[1] * scale_one + second[1] * scale_two
    weighted = first[2] * scale_one[..., None] + second[2] * scale_two[..., None]
    return (top, totals, weighted)


def partial_softmax(q_heads, k_heads, v_heads, bias, scale):
    scores = jnp.einsum("ihd,jhd->ihj", q_heads, k_heads, precision=HIGH) * scale + bias
    top = jnp.max(scores, axis=2)
    expo = jnp.exp(scores - top[..., None])
    totals = jnp.sum(expo, axis=2)
    weighted = jnp.einsum("ihj,jhd->ihd", expo, v_heads, precision=HIGH)
    return (top, totals, weighted)


def per_device(
    seq, query, key, value, pair, w_bias, w_out, w_left, w_right, w_outer, outer_bias, w_up, w_down
):
    rows_here = pair.shape[0]
    cols_here = pair.shape[1]
    channels = pair.shape[2]
    heads = w_bias.shape[1]
    width = w_out.shape[0]
    head_dim = width // heads
    proj_width = w_left.shape[1]
    scale = 1.0 / jnp.sqrt(jnp.float32(head_dim))
    bias = jnp.einsum("ijc,ch->ihj", channel_norm(pair), w_bias, precision=HIGH)
    queries = lax.all_gather(query, "col", axis=1, tiled=True)
    keys_all, values_all = (
        lax.all_gather(key, "row", axis=1, tiled=True),
        lax.all_gather(value, "row", axis=1, tiled=True),
    )
    parts = partial_softmax(
        queries.reshape(rows_here, heads, head_dim),
        keys_all.reshape(cols_here, heads, head_dim),
        values_all.reshape(cols_here, heads, head_dim),
        bias,
        scale,
    )
    top, totals, weighted = merged(parts, "col", combine)
    attn = (weighted / totals[..., None]).reshape(rows_here, width)
    seq_new = seq + jnp.dot(attn, w_out, precision=HIGH)
    sum_value, sum_square = lax.psum(
        (jnp.sum(seq_new, axis=1), jnp.sum(seq_new * seq_new, axis=1)), "col"
    )
    mean_value = (sum_value / width)[:, None]
    mean_square = (sum_square / width)[:, None]
    seq_norm = (seq_new - mean_value) * lax.rsqrt(mean_square - mean_value * mean_value + 1e-05)
    left_part = jnp.dot(seq_norm, w_left, precision=HIGH)
    right_part = jnp.dot(seq_norm, w_right, precision=HIGH)
    left, right = lax.psum((left_part, right_part), "col")
    right_every = lax.all_gather(right, "row", axis=0, tiled=True)
    start = lax.axis_index("col") * cols_here
    right_block = lax.dynamic_slice_in_dim(right_every, start, cols_here, 0)
    w_prod = w_outer[:proj_width]
    w_diff = w_outer[proj_width:]
    table = right_block[:, :, None] * w_prod[None, :, :]
    left_diff = jnp.dot(left, w_diff, precision=HIGH)
    right_diff = jnp.dot(right_block, w_diff, precision=HIGH)
    outer = (
        jnp.einsum("ip,jpc->ijc", left, table, precision=HIGH)
        + left_diff[:, None, :]
        - right_diff[None, :, :]
        + outer_bias
    )
    pair_mid = pair + outer
    flat = pair_mid.reshape(rows_here * cols_here, channels)
    hidden_act = jax.nn.relu(jnp.dot(channel_norm(flat), w_up, precision=HIGH))
    pair_new = flat + jnp.dot(hidden_act, w_down, precision=HIGH)
    return (seq_new, pair_new.reshape(rows_here, cols_here, channels))


def solution(mesh):
    in_specs = (
        P("row", "col"),
        P("row", "col"),
        P("col", "row"),
        P("col", "row"),
        P("row", "col", None),
        P(),
        P(None, "col"),
        P("col", None),
        P("col", None),
        P(),
        P(),
        P(),
        P(),
    )
    out_specs = (P("row", "col"), P("row", "col", None))
    return jax.shard_map(
        per_device, mesh=mesh, in_specs=in_specs, out_specs=out_specs, check_vma=False
    )
```

profile of v0, /device:TPU:0, one launch (start us, length us, event | category | flops | bytes accessed | tf_op | source)
XLA Modules:
  0.0 295.0 jit_solution(9783816739350070599)
XLA Ops:
  8.7 6.7 %all_gather.31 = f32[48,1024]{1,0:T(8,128)S(1)} all-gather(f32[48,512]{1,0:T(8,128)} %param.14), channel_id=1, replica_groups=mesh['row'=16,'col'=2] {'col'}, dimensions={1}, use_global_device_ids=true | all-gather | bytes 294912 | tf_op jit(solution)/shard_map/all_gather | solution.py:54
  15.6 6.2 %reduce_sum.63 = f32[48,384]{1,0:T(8,128)S(1)} reduce(f32[48,384,128]{2,1,0:T(8,128)} %param.17, f32[]{:T(128)} %constant.13.clone.1), dimensions={2}, to_apply=%region_0.0 | reduce | flops 2340864 | bytes 9510916 | tf_op jit(solution)/shard_map/reduce_sum | solution.py:20
  21.8 7.7 %multiply_reduce_fusion.1 = f32[48,384]{1,0:T(8,128)S(1)} fusion(f32[48,384,128]{2,1,0:T(8,128)} %param.17, f32[48,384]{1,0:T(8,128)S(1)} %broadcast_multiply_fusion.1), kind=kLoop, calls=%fused_computation.12 | loop fusion | flops 7059456 | bytes 9584640 | tf_op jit(solution)/shard_map/reduce_sum | solution.py:21
  29.5 15.9 %fusion.9 = f32[48,384,32]{1,2,0:T(8,128)} fusion(f32[48,384,128]{2,1,0:T(8,128)} %param.17, f32[48,384]{1,0:T(8,128)S(1)} %add_rsqrt_fusion.1, f32[48,384]{1,0:T(8,128)S(1)} %broadcast_multiply_fusion.1, f32[128,32]{0,1:T(8,128)S(1)} %copy-done.7), kind=kOutput, calls=%fused_computation.10 | convolution fusion | flops 910688256 | bytes 11960320 | tf_op jit(solution)/shard_map/ijc,ch->ihj/dot_general | solution.py:53
  45.4 7.2 %all-gather.8.cloned.1.call-done = f32[384,1024]{0,1:T(8,128)} async-done(((f32[384,64]{0,1:T(8,128)}), f32[384,1024]{0,1:T(8,128)}) %all-gather.8.cloned.1.call-update) | async-done | bytes 1572880 | tf_op jit(solution)/shard_map/all_gather | solution.py:56
  52.6 5.7 %fusion.45 = (f32[48,32]{0,1:T(8,128)S(1)}, f32[48,32,384]{2,0,1:T(8,128)S(1)}) fusion(f32[48,384,32]{1,2,0:T(8,128)} %fusion.9, f32[384,32,32]{0,2,1:T(8,128)} %bitcast.72, f32[48,32,32]{0,2,1:T(8,128)S(1)} %bitcast.70), kind=kOutput, calls=%fused_computation.63 | convolution fusion | flops 228260352 | bytes 6494208 | tf_op jit(solution)/shard_map/ihd,jhd->ihj/dot_general | solution.py:34
  58.3 1.4 copy-done.2
  60.5 32.7 %all-gather.10.cloned.1.call-done = f32[384,1024]{0,1:T(8,128)} async-done(((f32[384,64]{0,1:T(8,128)}), f32[384,1024]{0,1:T(8,128)}) %all-gather.10.cloned.1.call-update) | async-done | bytes 1572880 | tf_op jit(solution)/shard_map/all_gather | solution.py:57
  93.3 5.1 %fusion.20 = f32[48,32,32]{0,2,1:T(8,128)S(1)} fusion(f32[384,32,32]{0,2,1:T(8,128)} %bitcast.71, f32[48,32,384]{2,0,1:T(8,128)} %copy-done.2, f32[48,32]{0,1:T(8,128)S(1)} %get-tuple-element.37), kind=kOutput, calls=%fused_computation.22 | convolution fusion | flops 227082240 | bytes 4134912 | tf_op jit(solution)/shard_map/ihj,jhd->ihd/dot_general | solution.py:38
  98.3 4.4 %all-gather.3 = f32[2,48,32]{1,2,0:T(8,128)S(1)} all-gather(f32[1,48,32]{1,2,0:T(8,128)S(1)} %bitcast.73), channel_id=3, replica_groups=mesh['row'=16,'col'=2] {'col'}, dimensions={0}, use_global_device_ids=true | all-gather | bytes 18432 | tf_op jit(solution)/shard_map/all_gather | solution.py:10
  102.8 4.4 %all-gather.4 = f32[2,48,32]{1,2,0:T(8,128)S(1)} all-gather(f32[1,48,32]{1,2,0:T(8,128)S(1)} %bitcast.74), channel_id=4, replica_groups=mesh['row'=16,'col'=2] {'col'}, dimensions={0}, use_global_device_ids=true | all-gather | bytes 18432 | tf_op jit(solution)/shard_map/all_gather | solution.py:10
  108.7 18.0 %all-gather = f32[96,32,32]{2,1,0:T(8,128)S(1)} all-gather(f32[48,32,32]{2,1,0:T(8,128)S(1)} %copy.51), channel_id=2, replica_groups=mesh['row'=16,'col'=2] {'col'}, dimensions={0}, use_global_device_ids=true | all-gather | bytes 589824 | tf_op jit(solution)/shard_map/all_gather | solution.py:10
  126.8 2.0 fusion.23
  129.2 2.3 fusion.42
  131.5 4.9 %all-reduce.1 = (f32[48]{0:T(128)S(1)}, f32[48]{0:T(128)S(1)}) all-reduce(f32[48]{0:T(128)S(1)} %get-tuple-element.19, f32[48]{0:T(128)S(1)} %get-tuple-element.18), channel_id=1, replica_groups=mesh['row'=16,'col'=2] {'col'}, use_global_device_ids=true, to_apply=%region_7.0 | all-reduce | flops 96 | bytes 768 | tf_op jit(solution)/shard_map/psum | solution.py:69
  136.5 1.2 fusion.24
  138.9 8.6 %all-reduce = (f32[48,64]{1,0:T(8,128)S(1)}, f32[48,64]{1,0:T(8,128)S(1)}) all-reduce(f32[48,64]{1,0:T(8,128)S(1)} %fusion.24, f32[48,64]{1,0:T(8,128)S(1)} %fusion.25), channel_id=1, replica_groups=mesh['row'=16,'col'=2] {'col'}, use_global_device_ids=true, to_apply=%region_9.0 | all-reduce | flops 6144 | bytes 49152 | tf_op jit(solution)/shard_map/psum | solution.py:77
  147.6 20.2 %all_gather.39 = f32[768,64]{1,0:T(8,128)S(1)} all-gather(f32[48,64]{1,0:T(8,128)S(1)} %get-tuple-element.20), channel_id=1, replica_groups=mesh['row'=16,'col'=2] {'row'}, dimensions={0}, use_global_device_ids=true | all-gather | bytes 208896 | tf_op jit(solution)/shard_map/all_gather | solution.py:78
  168.2 22.6 %fusion.46 = (f32[48,384]{0,1:T(8,128)S(1)}, f32[48,384,128]{2,0,1:T(8,128)}) fusion(f32[128]{0:T(128)S(1)} %copy-done.8, f32[384,128]{1,0:T(8,128)S(1)} %fusion.30, f32[48,128]{1,0:T(8,128)S(1)} %fusion.32, f32[64,128]{1,0:T(8,128)S(1)} %slice-done.6, f32[384,64]{1,0:T(8,128)S(1)} %constant_dynamic-slice_fusion, f32[48,64]{1,0:T(8,128)S(1)} %get-tuple-element.21, ...), kind=kOutput, calls=%fused_computation.64 | convolution fusion | flops 1826863104 | bytes 19313152 | tf_op jit(solution)/shard_map/ip,jpc->ijc/dot_general | solution.py:87
  191.1 10.5 %copy.56 = f32[48,384,128]{2,1,0:T(8,128)} copy(f32[48,384,128]{2,0,1:T(8,128)} %get-tuple-element.41) | data formatting | bytes 18874368 | tf_op jit(solution)/shard_map/add | solution.py:92
  201.6 5.4 %multiply_reduce_fusion = f32[48,384]{0,1:T(8,128)S(1)} fusion(f32[48,384,128]{2,0,1:T(8,128)S(1)} %bitcast.65, f32[48,384]{0,1:T(8,128)S(1)} %copy.58), kind=kLoop, calls=%fused_computation.9 | loop fusion | flops 7059456 | bytes 9584640 | tf_op jit(solution)/shard_map/reduce_sum | solution.py:21
  207.2 11.4 %fusion.8 = f32[18432,128]{1,0:T(8,128)S(1)} fusion(f32[48,384,128]{2,1,0:T(8,128)} %copy.56, f32[18432]{0:T(1024)S(1)} %rsqrt.26, f32[18432]{0:T(1024)S(1)} %div.39), kind=kLoop, calls=%fused_computation.7 | loop fusion | flops 4718592 | bytes 19021824 | tf_op jit(solution)/shard_map/mul | solution.py:21
  218.6 33.8 %fusion.47 = f32[18432,512]{1,0:T(8,128)} fusion(f32[18432,128]{1,0:T(8,128)S(1)} %fusion.8, f32[128,512]{1,0:T(8,128)S(1)} %copy-done.5), kind=kOutput, calls=%fused_computation.65 | convolution fusion | flops 14495514624 | bytes 47448064 | tf_op jit(solution)/shard_map/dot_general | solution.py:94
  252.4 35.4 %fusion.2 = f32[18432,128]{1,0:T(8,128)} fusion(f32[18432,128]{1,0:T(8,128)S(1)} %bitcast.68, f32[512,128]{1,0:T(8,128)S(1)} %copy-done.6, f32[18432,512]{1,0:T(8,128)} %fusion.47), kind=kOutput, calls=%fused_computation.2 | convolution fusion | flops 14507311104 | bytes 56885248 | tf_op jit(solution)/shard_map/dot_general | solution.py:95
  (59 shorter events, 6.6 us)
Async XLA Ops:
  7.2 122.0 %copy-start = (f32[1024,512]{1,0:T(8,128)S(1)}, f32[1024,512]{1,0:T(8,128)}, u32[]{:S(2)}) copy-start(f32[1024,512]{1,0:T(8,128)} %param.19) | copy-start | bytes 6291460
  7.2 45.5 %all-gather.8.cloned.1.call-start = ((), (), s32[]{:S(2)}) async-start(), calls=%async_computation | async-start | bytes 1671168 | tf_op jit(solution)/shard_map/all_gather | solution.py:56
  7.9 85.3 %all-gather.10.cloned.1.call-start = ((), (), s32[]{:S(2)}) async-start(), calls=%async_computation.1 | async-start | bytes 1671168 | tf_op jit(solution)/shard_map/all_gather | solution.py:57
  15.6 14.0 %copy-start.7 = (f32[128,32]{0,1:T(8,128)S(1)}, f32[128,32]{0,1:T(8,128)}, u32[]{:S(2)}) copy-start(f32[128,32]{0,1:T(8,128)} %param.18) | copy-start | bytes 49156
  58.3 1.4 copy-start.2
  58.3 89.2 %copy-start.4 = (f32[128,128]{1,0:T(8,128)S(1)}, f32[128,128]{1,0:T(8,128)}, u32[]{:S(2)}) copy-start(f32[128,128]{1,0:T(8,128)} %param.22) | copy-start | bytes 196612
  58.3 109.8 %slice-start.6 = ((f32[128,128]{1,0:T(8,128)}), f32[64,128]{1,0:T(8,128)S(1)}, s32[]{:S(2)}) async-start(f32[128,128]{1,0:T(8,128)} %param.22), calls=%async_computation.8 | async-start | bytes 65536 | tf_op jit(solution)/shard_map/slice | solution.py:81
  108.7 59.4 %copy-start.8 = (f32[128]{0:T(128)S(1)}, f32[128]{0:T(128)}, u32[]{:S(2)}) copy-start(f32[128]{0:T(128)} %param.23) | copy-start | bytes 1540
  131.5 59.3 %copy-start.3 = (f32[48,512]{1,0:T(8,128)}, f32[48,512]{1,0:T(8,128)S(1)}, u32[]{:S(2)}) copy-start(f32[48,512]{1,0:T(8,128)S(1)} %get-tuple-element.39) | copy-start | bytes 294916
  190.9 10.6 %slice-start = ((s8[9437184]{0:T(1024)(128)(4,1)}), s8[1048576]{0:T(1024)(128)(4,1)S(1)}, s32[]{:S(2)}) async-start(s8[9437184]{0:T(1024)(128)(4,1)} %bitcast.64), calls=%async_computation.2 | async-start | bytes 2097152
  191.1 10.5 %slice-start.1 = ((s8[9437184]{0:T(1024)(128)(4,1)}), s8[4194304]{0:T(1024)(128)(4,1)S(1)}, s32[]{:S(2)}) async-start(s8[9437184]{0:T(1024)(128)(4,1)} %bitcast.64), calls=%async_computation.3 | async-start | bytes 8388608
  191.1 10.5 %slice-start.2 = ((s8[9437184]{0:T(1024)(128)(4,1)}), s8[4194304]{0:T(1024)(128)(4,1)S(1)}, s32[]{:S(2)}) async-start(s8[9437184]{0:T(1024)(128)(4,1)} %bitcast.64), calls=%async_computation.4 | async-start | bytes 8388608
  207.1 11.4 %copy-start.5 = (f32[128,512]{1,0:T(8,128)S(1)}, f32[128,512]{1,0:T(8,128)}, u32[]{:S(2)}) copy-start(f32[128,512]{1,0:T(8,128)} %param.24) | copy-start | bytes 786436
  207.2 45.3 %slice-start.3 = ((s8[9437184]{0:T(1024)(128)(4,1)}), s8[4194304]{0:T(1024)(128)(4,1)S(1)}, s32[]{:S(2)}) async-start(s8[9437184]{0:T(1024)(128)(4,1)} %bitcast.66), calls=%async_computation.5 | async-start | bytes 8388608
  218.6 33.8 %slice-start.4 = ((s8[9437184]{0:T(1024)(128)(4,1)}), s8[4194304]{0:T(1024)(128)(4,1)S(1)}, s32[]{:S(2)}) async-start(s8[9437184]{0:T(1024)(128)(4,1)} %bitcast.66), calls=%async_computation.6 | async-start | bytes 8388608
  218.6 33.8 %slice-start.5 = ((s8[9437184]{0:T(1024)(128)(4,1)}), s8[1048576]{0:T(1024)(128)(4,1)S(1)}, s32[]{:S(2)}) async-start(s8[9437184]{0:T(1024)(128)(4,1)} %bitcast.66), calls=%async_computation.7 | async-start | bytes 2097152
  218.6 33.8 %copy-start.6 = (f32[512,128]{1,0:T(8,128)S(1)}, f32[512,128]{1,0:T(8,128)}, u32[]{:S(2)}) copy-start(f32[512,128]{1,0:T(8,128)} %param.25) | copy-start | bytes 786436
  252.4 35.5 %copy-start.1 = (f32[1024,512]{1,0:T(8,128)S(1)}, f32[1024,512]{1,0:T(8,128)}, u32[]{:S(2)}) copy-start(f32[1024,512]{1,0:T(8,128)} %param.19) | copy-start | bytes 6291460
Sparse Core Ops, SparseCore 0:
  10.3 42.3 all-gather.7
  54.9 38.2 all-gather.9
where the time goes:
time: 298 us; the launch traced here: 295 us
  matrix products  124 us (42%)
  blocking collectives  67.2 us (23%)
  waiting for transfers between devices  41.3 us (14%)
  other arithmetic  33.6 us (11%)
  between operations  14.6 us (5%)
  local copies, waits for them, and re-layouts  14.4 us (5%)
    dot_general x1, matrix products, per_device(): pair_new = flat + jnp.dot(hidden_act, w_down, precision=HIGH)  35.4 us
    dot_general x1, matrix products, per_device(): hidden_act = jax.nn.relu(jnp.dot(channel_norm(flat), w_up, precision=HIGH))  33.8 us
    all_gather x1, waiting for transfers between devices, per_device(): lax.all_gather(value, 'row', axis=1, tiled=True)  32.7 us
    all_gather x3, blocking collectives, merged(): everything = jax.tree.map(lambda part: lax.all_gather(part, axis), x)  26.8 us
    dot_general x1, matrix products, per_device(): jnp.einsum('ip,jpc->ijc', left, table, precision=HIGH)  22.6 us
    all_gather x1, blocking collectives, per_device(): right_every = lax.all_gather(right, 'row', axis=0, tiled=True)  20.2 us
    dot_general x1, matrix products, per_device(): bias = jnp.einsum('ijc,ch->ihj', channel_norm(pair), w_bias, precision=HIGH)  15.9 us
    reduce_sum x2, other arithmetic, channel_norm(): jnp.mean(centre * centre, axis=-1, keepdims=True) + 1e-05  13.1 us
  transfers between devices with their start and end apart: 2, of which 2 were waited for; matrix products, arithmetic and copies ran while one was open for 12% of the time, Pallas kernels for 0%

commit v1 on v0

--- a/solution.py
+++ b/solution.py
@@ -42,6 +42,13 @@
 def per_device(
     seq, query, key, value, pair, w_bias, w_out, w_left, w_right, w_outer, outer_bias, w_up, w_down
 ):
+
+    def lane_link(local, peer_axis):
+        right_arr = jnp.stack(tuple((local for _ in range(jax.lax.axis_size(peer_axis)))), axis=0)
+        z_new = jax.lax.all_to_all(right_arr, peer_axis, 0, 0)
+        tile_out = jnp.concatenate(z_new, axis=1)
+        return tile_out
+
     rows_here = pair.shape[0]
     cols_here = pair.shape[1]
     channels = pair.shape[2]
@@ -52,10 +59,7 @@
     scale = 1.0 / jnp.sqrt(jnp.float32(head_dim))
     bias = jnp.einsum("ijc,ch->ihj", channel_norm(pair), w_bias, precision=HIGH)
     queries = lax.all_gather(query, "col", axis=1, tiled=True)
-    keys_all, values_all = (
-        lax.all_gather(key, "row", axis=1, tiled=True),
-        lax.all_gather(value, "row", axis=1, tiled=True),
-    )
+    keys_all, values_all = (lax.all_gather(key, "row", axis=1, tiled=True), lane_link(value, "row"))
     parts = partial_softmax(
         queries.reshape(rows_here, heads, head_dim),
         keys_all.reshape(cols_here, heads, head_dim),

time: 298 us -> 282 us (0.946)
  waiting for transfers between devices: 41.3 us -> 14.9 us
  starting transfers between devices: 0.08 us -> 7.5 us
    all_gather x1 -> x0, waiting for transfers between devices: 32.7 us -> none  [per_device(): lax.all_gather(value, 'row', axis=1, tiled=True)]
    all_to_all x0 -> x1, starting transfers between devices: none -> 7.46 us  [lane_link(): z_new = jax.lax.all_to_all(right_arr, peer_axis, 0, 0)]
    all_gather x1, waiting for transfers between devices: 7.2 us -> 14.3 us  [per_device(): lax.all_gather(key, 'row', axis=1, tiled=True)]
  transfers between devices with their start and end apart: 2 -> 2, of which waited for: 2 -> 1; matrix products, arithmetic and copies ran while one was open for 12% -> 14% of each run, Pallas kernels for 0% -> 0%
where the time goes in v1:
time: 282 us; the launch traced here: 279 us
  matrix products  124 us (44%)
  blocking collectives  68.1 us (24%)
  other arithmetic  33.6 us (12%)
  local copies, waits for them, and re-layouts  16.6 us (6%)
  waiting for transfers between devices  14.9 us (5%)
  between operations  14.7 us (5%)
  starting transfers between devices  7.5 us (3%)
    dot_general x1, matrix products, per_device(): pair_new = flat + jnp.dot(hidden_act, w_down, precision=HIGH)  35.4 us
    dot_general x1, matrix products, per_device(): hidden_act = jax.nn.relu(jnp.dot(channel_norm(flat), w_up, precision=HIGH))  33.8 us
    all_gather x3, blocking collectives, merged(): everything = jax.tree.map(lambda part: lax.all_gather(part, axis), x)  26.8 us
    dot_general x1, matrix products, per_device(): jnp.einsum('ip,jpc->ijc', left, table, precision=HIGH)  22.6 us
    all_gather x1, blocking collectives, per_device(): right_every = lax.all_gather(right, 'row', axis=0, tiled=True)  21.9 us
    dot_general x1, matrix products, per_device(): bias = jnp.einsum('ijc,ch->ihj', channel_norm(pair), w_bias, precision=HIGH)  15.9 us
    all_gather x1, waiting for transfers between devices, per_device(): lax.all_gather(key, 'row', axis=1, tiled=True)  14.3 us
    reduce_sum x2, other arithmetic, channel_norm(): jnp.mean(centre * centre, axis=-1, keepdims=True) + 1e-05  13.1 us
  transfers between devices with their start and end apart: 2, of which 1 were waited for; matrix products, arithmetic and copies ran while one was open for 14% of the time, Pallas kernels for 0%

profile of v1, /device:TPU:0, one launch (start us, length us, event | category | flops | bytes accessed | tf_op | source)
XLA Modules:
  0.0 279.2 jit_solution(5476236801310386444)
XLA Ops:
  7.9 2.2 stack.2
  10.1 7.5 %all-to-all-start = ((f32[16,384,64]{1,2,0:T(8,128)}), f32[16,384,64]{1,2,0:T(8,128)}, u32[]{:S(2)}, u32[]{:S(2)}) async-start(f32[16,384,64]{1,2,0:T(8,128)} %stack.2), calls=%async_computation | async-start | bytes 3145728 | tf_op jit(solution)/shard_map/all_to_all | solution.py:48
  17.6 5.9 %all_gather.28 = f32[48,1024]{1,0:T(8,128)S(1)} all-gather(f32[48,512]{1,0:T(8,128)} %param.14), channel_id=1, replica_groups=mesh['row'=16,'col'=2] {'col'}, dimensions={1}, use_global_device_ids=true | all-gather | bytes 294912 | tf_op jit(solution)/shard_map/all_gather | solution.py:61
  23.7 6.2 %reduce_sum.63 = f32[48,384]{1,0:T(8,128)S(1)} reduce(f32[48,384,128]{2,1,0:T(8,128)} %param.17, f32[]{:T(128)} %constant.13.clone.1), dimensions={2}, to_apply=%region_0.0 | reduce | flops 2340864 | bytes 9510916 | tf_op jit(solution)/shard_map/reduce_sum | solution.py:20
  29.9 7.7 %multiply_reduce_fusion.1 = f32[48,384]{1,0:T(8,128)S(1)} fusion(f32[48,384,128]{2,1,0:T(8,128)} %param.17, f32[48,384]{1,0:T(8,128)S(1)} %broadcast_multiply_fusion.1), kind=kLoop, calls=%fused_computation.12 | loop fusion | flops 7059456 | bytes 9584640 | tf_op jit(solution)/shard_map/reduce_sum | solution.py:21
  37.7 15.9 %fusion.9 = f32[48,384,32]{1,2,0:T(8,128)} fusion(f32[48,384,128]{2,1,0:T(8,128)} %param.17, f32[48,384]{1,0:T(8,128)S(1)} %add_rsqrt_fusion.1, f32[48,384]{1,0:T(8,128)S(1)} %broadcast_multiply_fusion.1, f32[128,32]{0,1:T(8,128)S(1)} %copy-done.7), kind=kOutput, calls=%fused_computation.10 | convolution fusion | flops 910688256 | bytes 11960320 | tf_op jit(solution)/shard_map/ijc,ch->ihj/dot_general | solution.py:60
  53.6 14.3 %all-gather.7.cloned.1.call-done = f32[384,1024]{0,1:T(8,128)} async-done(((f32[384,64]{0,1:T(8,128)}), f32[384,1024]{0,1:T(8,128)}) %all-gather.7.cloned.1.call-update) | async-done | bytes 1572880 | tf_op jit(solution)/shard_map/all_gather | solution.py:62
  67.9 5.7 %fusion.45 = (f32[48,32]{0,1:T(8,128)S(1)}, f32[48,32,384]{2,0,1:T(8,128)S(1)}) fusion(f32[48,384,32]{1,2,0:T(8,128)} %fusion.9, f32[384,32,32]{0,2,1:T(8,128)} %bitcast.73, f32[48,32,32]{0,2,1:T(8,128)S(1)} %bitcast.72), kind=kOutput, calls=%fused_computation.63 | convolution fusion | flops 228260352 | bytes 6494208 | tf_op jit(solution)/shard_map/ihd,jhd->ihj/dot_general | solution.py:34
  73.6 1.4 copy-done.2
  75.8 5.1 %fusion.20 = f32[48,32,32]{0,2,1:T(8,128)S(1)} fusion(f32[384,32,32]{0,2,1:T(8,128)} %bitcast.6, f32[48,32,384]{2,0,1:T(8,128)} %copy-done.2, f32[48,32]{0,1:T(8,128)S(1)} %get-tuple-element.37), kind=kOutput, calls=%fused_computation.22 | convolution fusion | flops 227082240 | bytes 4134912 | tf_op jit(solution)/shard_map/ihj,jhd->ihd/dot_general | solution.py:38
  80.9 4.4 %all-gather.3 = f32[2,48,32]{1,2,0:T(8,128)S(1)} all-gather(f32[1,48,32]{1,2,0:T(8,128)S(1)} %bitcast.74), channel_id=3, replica_groups=mesh['row'=16,'col'=2] {'col'}, dimensions={0}, use_global_device_ids=true | all-gather | bytes 18432 | tf_op jit(solution)/shard_map/all_gather | solution.py:10
  85.3 4.4 %all-gather.4 = f32[2,48,32]{1,2,0:T(8,128)S(1)} all-gather(f32[1,48,32]{1,2,0:T(8,128)S(1)} %bitcast.75), channel_id=4, replica_groups=mesh['row'=16,'col'=2] {'col'}, dimensions={0}, use_global_device_ids=true | all-gather | bytes 18432 | tf_op jit(solution)/shard_map/all_gather | solution.py:10
  91.2 18.0 %all-gather = f32[96,32,32]{2,1,0:T(8,128)S(1)} all-gather(f32[48,32,32]{2,1,0:T(8,128)S(1)} %copy.51), channel_id=2, replica_groups=mesh['row'=16,'col'=2] {'col'}, dimensions={0}, use_global_device_ids=true | all-gather | bytes 589824 | tf_op jit(solution)/shard_map/all_gather | solution.py:10
  109.3 2.0 fusion.23
  111.7 2.3 fusion.42
  114.0 4.9 %all-reduce.1 = (f32[48]{0:T(128)S(1)}, f32[48]{0:T(128)S(1)}) all-reduce(f32[48]{0:T(128)S(1)} %get-tuple-element.19, f32[48]{0:T(128)S(1)} %get-tuple-element.18), channel_id=1, replica_groups=mesh['row'=16,'col'=2] {'col'}, use_global_device_ids=true, to_apply=%region_7.0 | all-reduce | flops 96 | bytes 768 | tf_op jit(solution)/shard_map/psum | solution.py:73
  121.4 8.6 %all-reduce = (f32[48,64]{1,0:T(8,128)S(1)}, f32[48,64]{1,0:T(8,128)S(1)}) all-reduce(f32[48,64]{1,0:T(8,128)S(1)} %fusion.24, f32[48,64]{1,0:T(8,128)S(1)} %fusion.25), channel_id=1, replica_groups=mesh['row'=16,'col'=2] {'col'}, use_global_device_ids=true, to_apply=%region_9.0 | all-reduce | flops 6144 | bytes 49152 | tf_op jit(solution)/shard_map/psum | solution.py:81
  130.2 21.9 %all_gather.35 = f32[768,64]{1,0:T(8,128)S(1)} all-gather(f32[48,64]{1,0:T(8,128)S(1)} %get-tuple-element.20), channel_id=1, replica_groups=mesh['row'=16,'col'=2] {'row'}, dimensions={0}, use_global_device_ids=true | all-gather | bytes 208896 | tf_op jit(solution)/shard_map/all_gather | solution.py:82
  152.4 22.6 %fusion.46 = (f32[48,384]{0,1:T(8,128)S(1)}, f32[48,384,128]{2,0,1:T(8,128)}) fusion(f32[128]{0:T(128)S(1)} %copy-done.8, f32[384,128]{1,0:T(8,128)S(1)} %fusion.30, f32[48,128]{1,0:T(8,128)S(1)} %fusion.32, f32[64,128]{1,0:T(8,128)S(1)} %slice-done.6, f32[384,64]{1,0:T(8,128)S(1)} %constant_dynamic-slice_fusion, f32[48,64]{1,0:T(8,128)S(1)} %get-tuple-element.21, ...), kind=kOutput, calls=%fused_computation.64 | convolution fusion | flops 1826863104 | bytes 19313152 | tf_op jit(solution)/shard_map/ip,jpc->ijc/dot_general | solution.py:91
  175.2 10.5 %copy.56 = f32[48,384,128]{2,1,0:T(8,128)} copy(f32[48,384,128]{2,0,1:T(8,128)} %get-tuple-element.41) | data formatting | bytes 18874368 | tf_op jit(solution)/shard_map/add | solution.py:96
  185.7 5.4 %multiply_reduce_fusion = f32[48,384]{0,1:T(8,128)S(1)} fusion(f32[48,384,128]{2,0,1:T(8,128)S(1)} %bitcast.67, f32[48,384]{0,1:T(8,128)S(1)} %copy.58), kind=kLoop, calls=%fused_computation.9 | loop fusion | flops 7059456 | bytes 9584640 | tf_op jit(solution)/shard_map/reduce_sum | solution.py:21
  191.3 11.4 %fusion.8 = f32[18432,128]{1,0:T(8,128)S(1)} fusion(f32[48,384,128]{2,1,0:T(8,128)} %copy.56, f32[18432]{0:T(1024)S(1)} %rsqrt.26, f32[18432]{0:T(1024)S(1)} %div.39), kind=kLoop, calls=%fused_computation.7 | loop fusion | flops 4718592 | bytes 19021824 | tf_op jit(solution)/shard_map/mul | solution.py:21
  202.8 33.8 %fusion.47 = f32[18432,512]{1,0:T(8,128)} fusion(f32[18432,128]{1,0:T(8,128)S(1)} %fusion.8, f32[128,512]{1,0:T(8,128)S(1)} %copy-done.5), kind=kOutput, calls=%fused_computation.65 | convolution fusion | flops 14495514624 | bytes 47448064 | tf_op jit(solution)/shard_map/dot_general | solution.py:98
  236.6 35.4 %fusion.2 = f32[18432,128]{1,0:T(8,128)} fusion(f32[18432,128]{1,0:T(8,128)S(1)} %bitcast.70, f32[512,128]{1,0:T(8,128)S(1)} %copy-done.6, f32[18432,512]{1,0:T(8,128)} %fusion.47), kind=kOutput, calls=%fused_computation.2 | convolution fusion | flops 14507311104 | bytes 56885248 | tf_op jit(solution)/shard_map/dot_general | solution.py:99
  (59 shorter events, 7.0 us)
Async XLA Ops:
  7.2 104.5 %copy-start = (f32[1024,512]{1,0:T(8,128)S(1)}, f32[1024,512]{1,0:T(8,128)}, u32[]{:S(2)}) copy-start(f32[1024,512]{1,0:T(8,128)} %param.19) | copy-start | bytes 6291460
  7.2 60.7 %all-gather.7.cloned.1.call-start = ((), (), s32[]{:S(2)}) async-start(), calls=%async_computation.1 | async-start | bytes 1671168 | tf_op jit(solution)/shard_map/all_gather | solution.py:62
  10.1 65.6 %all-to-all-start = ((f32[16,384,64]{1,2,0:T(8,128)}), f32[16,384,64]{1,2,0:T(8,128)}, u32[]{:S(2)}, u32[]{:S(2)}) async-start(f32[16,384,64]{1,2,0:T(8,128)} %stack.2), calls=%async_computation | async-start | bytes 3145728 | tf_op jit(solution)/shard_map/all_to_all | solution.py:48
  23.7 14.0 %copy-start.7 = (f32[128,32]{0,1:T(8,128)S(1)}, f32[128,32]{0,1:T(8,128)}, u32[]{:S(2)}) copy-start(f32[128,32]{0,1:T(8,128)} %param.18) | copy-start | bytes 49156
  73.5 1.4 copy-start.2
  73.5 56.4 %copy-start.4 = (f32[128,128]{1,0:T(8,128)S(1)}, f32[128,128]{1,0:T(8,128)}, u32[]{:S(2)}) copy-start(f32[128,128]{1,0:T(8,128)} %param.22) | copy-start | bytes 196612
  73.5 78.8 %slice-start.6 = ((f32[128,128]{1,0:T(8,128)}), f32[64,128]{1,0:T(8,128)S(1)}, s32[]{:S(2)}) async-start(f32[128,128]{1,0:T(8,128)} %param.22), calls=%async_computation.8 | async-start | bytes 65536 | tf_op jit(solution)/shard_map/slice | solution.py:85
  91.2 61.1 %copy-start.8 = (f32[128]{0:T(128)S(1)}, f32[128]{0:T(128)}, u32[]{:S(2)}) copy-start(f32[128]{0:T(128)} %param.23) | copy-start | bytes 1540
  114.0 60.9 %copy-start.3 = (f32[48,512]{1,0:T(8,128)}, f32[48,512]{1,0:T(8,128)S(1)}, u32[]{:S(2)}) copy-start(f32[48,512]{1,0:T(8,128)S(1)} %get-tuple-element.39) | copy-start | bytes 294916
  175.1 10.6 %slice-start = ((s8[9437184]{0:T(1024)(128)(4,1)}), s8[1048576]{0:T(1024)(128)(4,1)S(1)}, s32[]{:S(2)}) async-start(s8[9437184]{0:T(1024)(128)(4,1)} %bitcast.66), calls=%async_computation.2 | async-start | bytes 2097152
  175.2 10.5 %slice-start.1 = ((s8[9437184]{0:T(1024)(128)(4,1)}), s8[4194304]{0:T(1024)(128)(4,1)S(1)}, s32[]{:S(2)}) async-start(s8[9437184]{0:T(1024)(128)(4,1)} %bitcast.66), calls=%async_computation.3 | async-start | bytes 8388608
  175.2 10.5 %slice-start.2 = ((s8[9437184]{0:T(1024)(128)(4,1)}), s8[4194304]{0:T(1024)(128)(4,1)S(1)}, s32[]{:S(2)}) async-start(s8[9437184]{0:T(1024)(128)(4,1)} %bitcast.66), calls=%async_computation.4 | async-start | bytes 8388608
  191.3 11.4 %copy-start.5 = (f32[128,512]{1,0:T(8,128)S(1)}, f32[128,512]{1,0:T(8,128)}, u32[]{:S(2)}) copy-start(f32[128,512]{1,0:T(8,128)} %param.24) | copy-start | bytes 786436
  191.3 45.3 %slice-start.3 = ((s8[9437184]{0:T(1024)(128)(4,1)}), s8[4194304]{0:T(1024)(128)(4,1)S(1)}, s32[]{:S(2)}) async-start(s8[9437184]{0:T(1024)(128)(4,1)} %bitcast.68), calls=%async_computation.5 | async-start | bytes 8388608
  202.8 33.8 %slice-start.4 = ((s8[9437184]{0:T(1024)(128)(4,1)}), s8[4194304]{0:T(1024)(128)(4,1)S(1)}, s32[]{:S(2)}) async-start(s8[9437184]{0:T(1024)(128)(4,1)} %bitcast.68), calls=%async_computation.6 | async-start | bytes 8388608
  202.8 33.8 %slice-start.5 = ((s8[9437184]{0:T(1024)(128)(4,1)}), s8[1048576]{0:T(1024)(128)(4,1)S(1)}, s32[]{:S(2)}) async-start(s8[9437184]{0:T(1024)(128)(4,1)} %bitcast.68), calls=%async_computation.7 | async-start | bytes 2097152
  202.8 33.8 %copy-start.6 = (f32[512,128]{1,0:T(8,128)S(1)}, f32[512,128]{1,0:T(8,128)}, u32[]{:S(2)}) copy-start(f32[512,128]{1,0:T(8,128)} %param.25) | copy-start | bytes 786436
  236.6 35.5 %copy-start.1 = (f32[1024,512]{1,0:T(8,128)S(1)}, f32[1024,512]{1,0:T(8,128)}, u32[]{:S(2)}) copy-start(f32[1024,512]{1,0:T(8,128)} %param.19) | copy-start | bytes 6291460
Sparse Core Ops, SparseCore 0:
  10.3 57.5 all-gather.6
